TPU v7x, 32 devices: a whole 2x2x4 slice. The times are simulated.
32 devices in a mesh: mp: 2 (over x), width: 2 (over y), hidden: 8 (over z, core).
Axes of the slice: x: 2, y: 2, z: 4, core: 2. Of those that a mesh axis runs over, the one named last changes fastest.
Arguments:
- residual_in: bfloat16 [2, 512, 3584], P('mp', 'hidden'), may hold values from -6 to 6
- gate_weight: bfloat16 [2, 14336, 3584], P('mp', ('width', 'hidden')), may hold values from -0.09375 to 0.09375
- up_weight: bfloat16 [2, 14336, 3584], P('mp', ('width', 'hidden')), may hold values from -0.09375 to 0.09375
- down_weight: bfloat16 [2, 14336, 3584], P('mp', ('width', 'hidden')), may hold values from -0.046875 to 0.046875
- enc_weight: float32 [7168, 16384], P(('mp', 'width'), 'hidden'), may hold values from -0.0625 to 0.0625
- enc_bias: float32 [16384], P('hidden'), may hold values from -3 to 3
- dec_weight: float32 [16384, 7168], P('hidden', ('mp', 'width')), may hold values from -0.25 to 0.25
- dec_bias: float32 [7168], P(('mp', 'width')), may hold values from -2 to 2
Outputs:
- mlp_acts: bfloat16 [2, 512, 3584], P('mp', 'hidden', 'width')
- latents: float32 [512, 16384], P(None, 'hidden')
- grad_enc: float32 [7168, 16384], P(('mp', 'width'), 'hidden')
- grad_dec: float32 [16384, 7168], P('hidden', ('mp', 'width'))
- grad_enc_bias: float32 [16384], P('hidden')
- grad_dec_bias: float32 [7168], P(('mp', 'width'))
All inputs are finite; a program needn't handle non-finite values.
Results may differ from a plain program's by a relative error of at most 0.0058.
Values may be sent and summed in bfloat16 or wider, within the bound.
A program may use at most 192 MiB of HBM per device.

v0:
```python
import jax
import jax.numpy as jnp
from jax import lax
from jax.sharding import PartitionSpec as P

TOKENS = 512
sharpness = 8.0
sparsity_coef = 0.02
norm_floor = 1e-06
highest = lax.Precision.HIGHEST


def body(
    residual_in, gate_weight, up_weight, down_weight, enc_weight, enc_bias, dec_weight, dec_bias
):
    last_last = (((1,), (1,)), ((), ()))
    first_first = (((0,), (0,)), ((), ()))
    gathered = lax.all_gather(residual_in[0], "hidden", axis=0, tiled=True)
    gate_act = lax.dot_general(
        gathered, gate_weight[0], last_last, preferred_element_type=jnp.float32
    )
    up_act = lax.dot_general(gathered, up_weight[0], last_last, preferred_element_type=jnp.float32)
    hidden_act = (jax.nn.gelu(gate_act, approximate=True) * up_act).astype(jnp.bfloat16)
    down_local = down_weight[0]
    row_sums = lax.psum_scatter(
        jnp.dot(hidden_act, down_local, preferred_element_type=jnp.float32),
        "hidden",
        scatter_dimension=0,
        tiled=True,
    )
    model_sums = lax.psum_scatter(row_sums, "width", scatter_dimension=1, tiled=True)
    mlp_acts = model_sums.astype(jnp.bfloat16)
    coder_in = lax.all_gather(mlp_acts, "hidden", axis=0, tiled=True).astype(jnp.float32)
    enc_partial = jnp.dot(coder_in, enc_weight, precision=highest)
    model_index = lax.axis_index("mp")
    squares = jnp.sum(dec_weight * dec_weight, axis=1)
    square_pair = jnp.where(jnp.arange(2)[:, None] == model_index, squares[None, :], 0.0)
    pre_sum, square_sums = lax.psum((enc_partial, square_pair), ("mp", "width"))
    pre_act = pre_sum + enc_bias
    latents = jax.nn.softplus(sharpness * pre_act) / sharpness
    dec_norms = jnp.sqrt(square_sums + norm_floor)
    recon_part = jnp.dot(latents, dec_weight, precision=highest)
    own_rebuilt = lax.psum_scatter(recon_part, "hidden", scatter_dimension=0, tiled=True) + dec_bias
    own_grad = 2.0 / TOKENS * (own_rebuilt - mlp_acts.astype(jnp.float32))
    err_grad = lax.all_gather(own_grad.astype(jnp.bfloat16), "hidden", axis=0, tiled=True).astype(
        own_grad.dtype
    )
    grad_dec_bias = jnp.sum(err_grad, axis=0)
    back_part = lax.dot_general(
        err_grad, dec_weight, last_last, precision=highest, preferred_element_type=jnp.float32
    )
    lat_grad = lax.psum(back_part.astype(jnp.bfloat16), ("mp", "width")).astype(
        jnp.float32
    ) + sparsity_coef * (dec_norms[0] + dec_norms[1])
    pre_grad = lat_grad * jax.nn.sigmoid(sharpness * pre_act)
    grad_enc_bias = jnp.sum(pre_grad, axis=0)
    grad_enc = lax.dot_general(
        coder_in, pre_grad, first_first, precision=highest, preferred_element_type=jnp.float32
    )
    latent_totals = jnp.sum(latents, axis=0)
    own_norm = jnp.where(model_index == 0, dec_norms[0], dec_norms[1])
    grad_dec = lax.dot_general(
        latents, err_grad, first_first, precision=highest, preferred_element_type=jnp.float32
    )
    grad_dec = grad_dec + sparsity_coef * (latent_totals / own_norm)[:, None] * dec_weight
    return (mlp_acts[None], latents, grad_enc, grad_dec, grad_enc_bias, grad_dec_bias)


def solution(mesh):
    return jax.shard_map(
        body,
        mesh=mesh,
        in_specs=(
            P("mp", "hidden", None),
            P("mp", ("width", "hidden"), None),
            P("mp", ("width", "hidden"), None),
            P("mp", ("width", "hidden"), None),
            P(("mp", "width"), "hidden"),
            P("hidden"),
            P("hidden", ("mp", "width")),
            P(("mp", "width")),
        ),
        out_specs=(
            P("mp", "hidden", "width"),
            P(None, "hidden"),
            P(("mp", "width"), "hidden"),
            P("hidden", ("mp", "width")),
            P("hidden"),
            P(("mp", "width")),
        ),
        check_vma=False,
    )
```

profile of v0, /device:TPU:0, one launch (start us, length us, event | category | flops | bytes accessed | tf_op | source)
XLA Modules:
  0.0 549.1 jit_solution(14673929088239518730)
XLA Ops:
  7.2 0.0 all-gather.9.cloned.1.call-start
  7.2 0.7 all-gather.9.cloned.1.call-update
  7.9 0.0 reduce-scatter.4.cloned.1.call-start
  7.9 47.0 %all-gather.9.cloned.1.call-done = bf16[1,512,3584]{2,1,0:T(8,128)(2,1)} async-done(((bf16[1,64,3584]{2,1,0:T(8,128)(2,1)}), bf16[1,512,3584]{2,1,0:T(8,128)(2,1)}) %all-gather.9.cloned.1.call-update) | async-done | bytes 3670032 | tf_op jit(solution)/shard_map/all_gather | solution.py:18
  54.9 0.0 copy-start.7
  54.9 0.0 slice-start
  54.9 9.6 %fusion.4 = f32[512,896]{1,0:T(8,128)S(1)} fusion(bf16[1,896,3584]{2,1,0:T(8,128)(2,1)} %param.9, bf16[1,512,3584]{2,1,0:T(8,128)(2,1)} %all-gather.9.cloned.1.call-done), kind=kOutput, calls=%fused_computation.7 | convolution fusion | flops 3288334336 | bytes 11927552 | tf_op jit(solution)/shard_map/dot_general | solution.py:19
  64.5 0.0 copy-done.7
  64.6 0.0 slice-start.1
  64.6 7.1 %fusion.17 = bf16[512,896]{1,0:T(8,128)(2,1)S(1)} fusion(f32[512,896]{1,0:T(8,128)S(1)} %fusion.4, bf16[1,896,3584]{2,1,0:T(8,128)(2,1)} %param.10, bf16[1,512,3584]{2,1,0:T(8,128)(2,1)S(1)} %copy-done.7), kind=kOutput, calls=%fused_computation.25 | convolution fusion | flops 3292921856 | bytes 12845056 | tf_op jit(solution)/shard_map/dot_general | solution.py:22
  71.7 0.0 slice-done
  71.7 0.0 slice-done.1
  71.7 6.0 %fusion = f32[512,3584]{1,0:T(8,128)} fusion(bf16[512,896]{1,0:T(8,128)(2,1)S(1)} %fusion.17, bf16[1,896,3584]{2,1,0:T(8,128)(2,1)S(1)} %bitcast.36), kind=kOutput, calls=%fused_computation.3 | convolution fusion | flops 3288334336 | bytes 14680064 | tf_op jit(solution)/shard_map/dot_general | solution.py:26
  77.8 0.0 reduce-scatter.4.cloned.1.call-update
  77.8 0.0 reduce-scatter.6.cloned.1.call-start
  77.9 78.6 %reduce-scatter.4.cloned.1.call-done = f32[64,3584]{1,0:T(8,128)} async-done(((f32[512,3584]{1,0:T(8,128)}), f32[64,3584]{1,0:T(8,128)}) %reduce-scatter.4.cloned.1.call-update) | async-done | bytes 917520 | tf_op jit(solution)/shard_map/reduce_scatter | solution.py:25
  156.4 0.0 reduce-scatter.6.cloned.1.call-update
  156.4 0.0 all-gather.5.cloned.1.call-start
  156.5 19.6 %reduce-scatter.6.cloned.1.call-done = f32[64,1792]{1,0:T(8,128)} async-done(((f32[64,3584]{1,0:T(8,128)}), f32[64,1792]{1,0:T(8,128)}) %reduce-scatter.6.cloned.1.call-update) | async-done | bytes 458768 | tf_op jit(solution)/shard_map/reduce_scatter | solution.py:31
  176.1 1.7 convert_element_type.23
  177.8 0.0 all-gather.5.cloned.1.call-update
  177.9 0.3 all-reduce.3.cloned.1.call-start
  178.2 27.0 %all-gather.5.cloned.1.call-done = bf16[512,1792]{1,0:T(8,128)(2,1)} async-done(((bf16[64,1792]{1,0:T(8,128)(2,1)}), bf16[512,1792]{1,0:T(8,128)(2,1)}) %all-gather.5.cloned.1.call-update) | async-done | bytes 1835024 | tf_op jit(solution)/shard_map/all_gather | solution.py:33
  205.2 16.9 %fusion.26 = f32[512,2048]{1,0:T(8,128)} fusion(bf16[512,1792]{1,0:T(8,128)(2,1)} %all-gather.5.cloned.1.call-done, f32[1792,2048]{1,0:T(8,128)} %param.12), kind=kOutput, calls=%fused_computation.36 | convolution fusion | flops 22548578304 | bytes 20709376 | tf_op jit(solution)/shard_map/dot_general | solution.py:34
  222.1 0.0 copy-start.5
  222.1 0.0 all-reduce.3.cloned.1.call-update
  222.1 0.4 reduce-scatter.8.cloned.1.call-start
  222.5 102.8 %all-reduce.3.cloned.1.call-done = f32[512,2048]{1,0:T(8,128)} async-done(((f32[512,2048]{1,0:T(8,128)}), f32[512,2048]{1,0:T(8,128)}) %all-reduce.3.cloned.1.call-update) | async-done | bytes 4194320 | tf_op jit(solution)/shard_map/psum | solution.py:38
  325.3 0.0 copy-done.5
  325.3 4.9 fusion.24
  330.2 0.0 copy-start
  330.2 2.0 copy-done
  332.2 0.0 copy-start.3
  332.2 0.0 copy-start.6
  332.2 26.6 %fusion.27 = f32[512,1792]{1,0:T(8,128)} fusion(f32[512,2048]{1,0:T(8,128)S(1)} %get-tuple-element.7, f32[2048,1792]{1,0:T(8,128)} %param.14), kind=kOutput, calls=%fused_computation.37 | convolution fusion | flops 22548578304 | bytes 22544384 | tf_op jit(solution)/shard_map/dot_general | solution.py:42
  358.9 0.0 reduce-scatter.8.cloned.1.call-update
  358.9 0.0 all-gather.7.cloned.1.call-start
  359.0 45.1 %reduce-scatter.8.cloned.1.call-done = f32[64,1792]{1,0:T(8,128)} async-done(((f32[512,1792]{1,0:T(8,128)}), f32[64,1792]{1,0:T(8,128)}) %reduce-scatter.8.cloned.1.call-update) | async-done | bytes 458768 | tf_op jit(solution)/shard_map/reduce_scatter | solution.py:43
  404.0 0.0 copy-done.3
  404.0 0.0 copy-done.6
  404.1 1.8 multiply_convert_fusion
  405.8 0.0 all-gather.7.cloned.1.call-update
  405.8 0.0 all-reduce.5.cloned.1.call-start
  405.9 6.2 %multiply_reduce_fusion = f32[2048]{0:T(1024)S(1)} fusion(f32[2048,1792]{1,0:T(8,128)} %param.14), kind=kLoop, calls=%fused_computation.1 | loop fusion | flops 7337984 | bytes 14688256 | tf_op jit(solution)/shard_map/reduce_sum | solution.py:36
  412.1 0.1 broadcast_select_fusion
  412.2 16.5 %psum.23 = f32[2,2048]{1,0:T(2,128)S(1)} all-reduce(f32[2,2048]{1,0:T(2,128)S(1)} %broadcast_select_fusion), channel_id=1, replica_groups=mesh['mp'=2,'width'=2,'hidden'=8] {'mp','width'}, use_global_device_ids=true, to_apply=%region_6.7 | all-reduce | flops 4096 | bytes 32768 | tf_op jit(solution)/shard_map/psum | solution.py:38
  428.8 2.9 all-gather.7.cloned.1.call-done
  431.7 0.0 copy-start.2
  431.7 18.4 %convolution_convert_fusion = bf16[512,2048]{1,0:T(8,128)(2,1)} fusion(bf16[512,1792]{1,0:T(8,128)(2,1)} %all-gather.7.cloned.1.call-done, f32[2048,1792]{1,0:T(8,128)} %param.14), kind=kOutput, calls=%fused_computation.15 | convolution fusion | flops 22549626880 | bytes 18612224 | tf_op jit(solution)/shard_map/dot_general | solution.py:49
  450.1 0.0 all-reduce.5.cloned.1.call-update
  450.1 0.7 convert_bitcast_fusion
  450.8 0.0 copy-done.2
  450.8 0.9 convert_reduce_fusion
  451.7 19.6 %multiply_add_fusion = f32[2048,1792]{1,0:T(8,128)} fusion(f32[2048,1792]{1,0:T(8,128)} %param.14, f32[512,2048]{1,0:T(8,128)} %copy-done, bf16[512,1792]{1,0:T(8,128)(2,1)S(1)} %copy-done.2, f32[2048]{0:T(1024)S(1)} %divide_multiply_fusion.1), kind=kOutput, calls=%fused_computation | convolution fusion | flops 22555918336 | bytes 35397632 | tf_op jit(solution)/shard_map/dot_general | solution.py:62
  471.3 47.8 %all-reduce.5.cloned.1.call-done = bf16[512,2048]{1,0:T(8,128)(2,1)} async-done(((bf16[512,2048]{1,0:T(8,128)(2,1)}), bf16[512,2048]{1,0:T(8,128)(2,1)}) %all-reduce.5.cloned.1.call-update) | async-done | bytes 2097168 | tf_op jit(solution)/shard_map/psum | solution.py:52
  519.1 0.0 copy-start.1
  519.1 0.0 copy-start.4
  519.2 5.0 fusion.22
  524.1 0.0 copy-done.1
  524.1 0.0 copy-done.4
  524.1 17.9 %fusion.23 = f32[1792,2048]{1,0:T(8,128)} fusion(bf16[512,1792]{1,0:T(8,128)(2,1)} %all-gather.5.cloned.1.call-done, bf16[512,2048]{1,0:T(8,128)(2,1)S(1)} %copy-done.4, f32[512,2048]{1,0:T(8,128)S(1)} %copy-done.1, f32[2048]{0:T(1024)S(1)} %bitcast.33, f32[2048]{0:T(1024)S(1)} %copy-done.5), kind=kOutput, calls=%fused_computation.34 | convolution fusion | flops 22556966912 | bytes 22822912 | tf_op jit(solution)/shard_map/dot_general | solution.py:57
  (5 shorter events, 0.1 us)
Async XLA Ops:
  7.2 47.7 %all-gather.9.cloned.1.call-start = ((), (), s32[]{:S(2)}) async-start(), calls=%async_computation.10 | async-start | bytes 4128768 | tf_op jit(solution)/shard_map/all_gather | solution.py:18
  7.9 148.5 %reduce-scatter.4.cloned.1.call-start = ((), (), s32[]{:S(2)}) async-start(), calls=%async_computation.3 | async-start | bytes 8257536 | tf_op jit(solution)/shard_map/reduce_scatter | solution.py:25
  54.9 9.6 %copy-start.7 = (bf16[1,512,3584]{2,1,0:T(8,128)(2,1)S(1)}, bf16[1,512,3584]{2,1,0:T(8,128)(2,1)}, u32[]{:S(2)}) copy-start(bf16[1,512,3584]{2,1,0:T(8,128)(2,1)} %all-gather.9.cloned.1.call-done) | copy-start | bytes 11010052
  54.9 16.8 %slice-start = ((s8[6422528]{0:T(1024)(128)(4,1)}), s8[4194304]{0:T(1024)(128)(4,1)S(1)}, s32[]{:S(2)}) async-start(s8[6422528]{0:T(1024)(128)(4,1)} %bitcast.35), calls=%async_computation.11 | async-start | bytes 8388608
  64.6 7.2 %slice-start.1 = ((s8[6422528]{0:T(1024)(128)(4,1)}), s8[2228224]{0:T(1024)(128)(4,1)S(1)}, s32[]{:S(2)}) async-start(s8[6422528]{0:T(1024)(128)(4,1)} %bitcast.35), calls=%async_computation.12 | async-start | bytes 4456448
  77.8 98.3 %reduce-scatter.6.cloned.1.call-start = ((), (), s32[]{:S(2)}) async-start(), calls=%async_computation.4 | async-start | bytes 1376256 | tf_op jit(solution)/shard_map/reduce_scatter | solution.py:31
  156.4 48.8 %all-gather.5.cloned.1.call-start = ((), (), s32[]{:S(2)}) async-start(), calls=%async_computation.5 | async-start | bytes 2064384 | tf_op jit(solution)/shard_map/all_gather | solution.py:33
  177.9 147.4 %all-reduce.3.cloned.1.call-start = ((), (), s32[]{:S(2)}) async-start(), calls=%async_computation.6 | async-start | bytes 8388608 | tf_op jit(solution)/shard_map/psum | solution.py:38
  222.1 103.2 %copy-start.5 = (f32[2048]{0:T(1024)S(1)}, f32[2048]{0:T(1024)}, u32[]{:S(2)}) copy-start(f32[2048]{0:T(1024)} %param.13) | copy-start | bytes 24580
  222.1 181.9 %reduce-scatter.8.cloned.1.call-start = ((), (), s32[]{:S(2)}) async-start(), calls=%async_computation.7 | async-start | bytes 4128768 | tf_op jit(solution)/shard_map/reduce_scatter | solution.py:43
  330.2 2.0 copy-start
  332.2 71.8 %copy-start.3 = (f32[64,1792]{1,0:T(8,128)S(1)}, f32[64,1792]{1,0:T(8,128)}, u32[]{:S(2)}) copy-start(f32[64,1792]{1,0:T(8,128)} %reduce-scatter.6.cloned.1.call-done) | copy-start | bytes 1376260
  332.2 71.8 %copy-start.6 = (f32[1792]{0:T(1024)S(1)}, f32[1792]{0:T(1024)}, u32[]{:S(2)}) copy-start(f32[1792]{0:T(1024)} %param.15) | copy-start | bytes 21508
  358.9 72.7 %all-gather.7.cloned.1.call-start = ((), (), s32[]{:S(2)}) async-start(), calls=%async_computation.8 | async-start | bytes 2064384 | tf_op jit(solution)/shard_map/all_gather | solution.py:45
  405.8 113.3 %all-reduce.5.cloned.1.call-start = ((), (), s32[]{:S(2)}) async-start(), calls=%async_computation.9 | async-start | bytes 4194304 | tf_op jit(solution)/shard_map/psum | solution.py:52
  431.7 19.2 %copy-start.2 = (bf16[512,1792]{1,0:T(8,128)(2,1)S(1)}, bf16[512,1792]{1,0:T(8,128)(2,1)}, u32[]{:S(2)}) copy-start(bf16[512,1792]{1,0:T(8,128)(2,1)} %all-gather.7.cloned.1.call-done) | copy-start | bytes 5505028
  519.1 5.0 copy-start.1
  519.1 5.0 copy-start.4
Sparse Core Ops, SparseCore 0:
  9.6 45.2 all-gather.8
  77.9 78.4 reduce-scatter.3
  158.7 17.3 reduce-scatter.5
  178.2 26.9 all-gather.4
  222.2 103.0 all-reduce.2
  359.0 44.9 reduce-scatter.7
  406.3 25.3 all-gather.6
  450.2 68.8 all-reduce.4
where the time goes:
time: 555 us; the launch traced here: 549 us
  waiting for transfers between devices  372 us (67%)
  matrix products  122 us (22%)
  other arithmetic  21.3 us (4%)
  blocking collectives  16.5 us (3%)
  between operations  14.5 us (3%)
    psum x1, waiting for transfers between devices, body(): pre_sum, square_sums = lax.psum((enc_partial, square_pair), ('mp', 'width'))  103 us
    reduce_scatter x1, waiting for transfers between devices, body(): lax.psum_scatter(jnp.dot(hidden_act, down_local, preferred_element_type=j...  78.6 us
    psum x1, waiting for transfers between devices, body(): lax.psum(back_part.astype(jnp.bfloat16), ('mp', 'width'))  47.8 us
    all_gather x1, waiting for transfers between devices, body(): gathered = lax.all_gather(residual_in[0], 'hidden', axis=0, tiled=True)  47 us
    reduce_scatter x1, waiting for transfers between devices, body(): lax.psum_scatter(recon_part, 'hidden', scatter_dimension=0, tiled=True)  45.1 us
    all_gather x1, waiting for transfers between devices, body(): lax.all_gather(mlp_acts, 'hidden', axis=0, tiled=True).astype(jnp.float32)  27 us
    dot_general x1, matrix products, body(): recon_part = jnp.dot(latents, dec_weight, precision=highest)  26.6 us
    reduce_scatter x1, waiting for transfers between devices, body(): lax.psum_scatter(row_sums, 'width', scatter_dimension=1, tiled=True)  19.6 us
  transfers between devices with their start and end apart: 8, of which 8 were waited for; matrix products, arithmetic and copies ran while one was open for 5% of the time, Pallas kernels for 0%

commit v1 on v0

--- a/solution.py
+++ b/solution.py
@@ -1,3 +1,4 @@
+import functools
 import jax
 import jax.numpy as jnp
 from jax import lax
@@ -8,6 +9,14 @@
 sparsity_coef = 0.02
 norm_floor = 1e-06
 highest = lax.Precision.HIGHEST
+
+
+def render_the_indices(block_here, axis_id):
+    block_last = lax.all_gather(block_here, axis_name=axis_id).sum(axis=0)
+    return block_last
+
+
+point_cubes_by_axis = functools.partial(render_the_indices, axis_id=("mp", "width"))
 
 
 def body(
@@ -49,7 +58,7 @@
     back_part = lax.dot_general(
         err_grad, dec_weight, last_last, precision=highest, preferred_element_type=jnp.float32
     )
-    lat_grad = lax.psum(back_part.astype(jnp.bfloat16), ("mp", "width")).astype(
+    lat_grad = point_cubes_by_axis(back_part.astype(jnp.bfloat16)).astype(
         jnp.float32
     ) + sparsity_coef * (dec_norms[0] + dec_norms[1])
     pre_grad = lat_grad * jax.nn.sigmoid(sharpness * pre_act)

time: 555 us -> 574 us (1.034)
  waiting for transfers between devices: 372 us -> 390 us
    psum x1 -> x0, waiting for transfers between devices: 47.8 us -> none  [body(): lax.psum(back_part.astype(jnp.bfloat16), ('mp', 'width'))]
    all_gather x0 -> x1, waiting for transfers between devices: none -> 43.3 us  [render_the_indices(): block_last = lax.all_gather(block_here, axis_name=axis_id).sum(axis=0)]
    all_gather x1, waiting for transfers between devices: 2.86 us -> 25.6 us  [body(): lax.all_gather(own_grad.astype(jnp.bfloat16), 'hidden', axis=0, tiled=True)]
where the time goes in v1:
time: 574 us; the launch traced here: 569 us
  waiting for transfers between devices  390 us (68%)
  matrix products  117 us (20%)
  other arithmetic  26.5 us (5%)
  blocking collectives  17.1 us (3%)
  between operations  14.8 us (3%)
    psum x1, waiting for transfers between devices, body(): pre_sum, square_sums = lax.psum((enc_partial, square_pair), ('mp', 'width'))  103 us
    reduce_scatter x1, waiting for transfers between devices, body(): lax.psum_scatter(jnp.dot(hidden_act, down_local, preferred_element_type=j...  78.6 us
    all_gather x1, waiting for transfers between devices, body(): gathered = lax.all_gather(residual_in[0], 'hidden', axis=0, tiled=True)  47 us
    reduce_scatter x1, waiting for transfers between devices, body(): lax.psum_scatter(recon_part, 'hidden', scatter_dimension=0, tiled=True)  45.1 us
    all_gather x1, waiting for transfers between devices, render_the_indices(): block_last = lax.all_gather(block_here, axis_name=axis_id).sum(axis=0)  43.3 us
    all_gather x1, waiting for transfers between devices, body(): lax.all_gather(mlp_acts, 'hidden', axis=0, tiled=True).astype(jnp.float32)  26.8 us
    dot_general x1, matrix products, body(): recon_part = jnp.dot(latents, dec_weight, precision=highest)  26.6 us
    all_gather x1, waiting for transfers between devices, body(): lax.all_gather(own_grad.astype(jnp.bfloat16), 'hidden', axis=0, tiled=True)  25.6 us
  transfers between devices with their start and end apart: 8, of which 8 were waited for; matrix products, arithmetic and copies ran while one was open for 5% of the time, Pallas kernels for 0%

profile of v1, /device:TPU:0, one launch (start us, length us, event | category | flops | bytes accessed | tf_op | source)
XLA Modules:
  0.0 568.7 jit_solution(1703292987378138539)
XLA Ops:
  7.2 0.0 all-gather.11.cloned.1.call-start
  7.2 0.7 all-gather.11.cloned.1.call-update
  7.9 0.0 reduce-scatter.4.cloned.1.call-start
  7.9 47.0 %all-gather.11.cloned.1.call-done = bf16[1,512,3584]{2,1,0:T(8,128)(2,1)} async-done(((bf16[1,64,3584]{2,1,0:T(8,128)(2,1)}), bf16[1,512,3584]{2,1,0:T(8,128)(2,1)}) %all-gather.11.cloned.1.call-update) | async-done | bytes 3670032 | tf_op jit(solution)/shard_map/all_gather | solution.py:27
  54.9 0.0 copy-start.6
  54.9 0.0 slice-start
  54.9 9.6 %fusion.4 = f32[512,896]{1,0:T(8,128)S(1)} fusion(bf16[1,896,3584]{2,1,0:T(8,128)(2,1)} %param.9, bf16[1,512,3584]{2,1,0:T(8,128)(2,1)} %all-gather.11.cloned.1.call-done), kind=kOutput, calls=%fused_computation.7 | convolution fusion | flops 3288334336 | bytes 11927552 | tf_op jit(solution)/shard_map/dot_general | solution.py:28
  64.5 0.0 copy-done.6
  64.6 0.0 slice-start.1
  64.6 7.1 %fusion.17 = bf16[512,896]{1,0:T(8,128)(2,1)S(1)} fusion(f32[512,896]{1,0:T(8,128)S(1)} %fusion.4, bf16[1,896,3584]{2,1,0:T(8,128)(2,1)} %param.10, bf16[1,512,3584]{2,1,0:T(8,128)(2,1)S(1)} %copy-done.6), kind=kOutput, calls=%fused_computation.25 | convolution fusion | flops 3292921856 | bytes 12845056 | tf_op jit(solution)/shard_map/dot_general | solution.py:31
  71.7 0.0 slice-done
  71.7 0.0 slice-done.1
  71.7 6.0 %fusion = f32[512,3584]{1,0:T(8,128)} fusion(bf16[512,896]{1,0:T(8,128)(2,1)S(1)} %fusion.17, bf16[1,896,3584]{2,1,0:T(8,128)(2,1)S(1)} %bitcast.38), kind=kOutput, calls=%fused_computation.3 | convolution fusion | flops 3288334336 | bytes 14680064 | tf_op jit(solution)/shard_map/dot_general | solution.py:35
  77.8 0.0 reduce-scatter.4.cloned.1.call-update
  77.8 0.0 reduce-scatter.6.cloned.1.call-start
  77.9 78.6 %reduce-scatter.4.cloned.1.call-done = f32[64,3584]{1,0:T(8,128)} async-done(((f32[512,3584]{1,0:T(8,128)}), f32[64,3584]{1,0:T(8,128)}) %reduce-scatter.4.cloned.1.call-update) | async-done | bytes 917520 | tf_op jit(solution)/shard_map/reduce_scatter | solution.py:34
  156.4 0.0 reduce-scatter.6.cloned.1.call-update
  156.4 0.0 all-gather.7.cloned.1.call-start
  156.5 19.6 %reduce-scatter.6.cloned.1.call-done = f32[64,1792]{1,0:T(8,128)} async-done(((f32[64,3584]{1,0:T(8,128)}), f32[64,1792]{1,0:T(8,128)}) %reduce-scatter.6.cloned.1.call-update) | async-done | bytes 458768 | tf_op jit(solution)/shard_map/reduce_scatter | solution.py:40
  176.1 1.7 convert_element_type.25
  177.8 0.0 all-gather.7.cloned.1.call-update
  177.9 0.6 all-reduce.2.cloned.1.call-start
  178.4 26.8 %all-gather.7.cloned.1.call-done = bf16[512,1792]{1,0:T(8,128)(2,1)} async-done(((bf16[64,1792]{1,0:T(8,128)(2,1)}), bf16[512,1792]{1,0:T(8,128)(2,1)}) %all-gather.7.cloned.1.call-update) | async-done | bytes 1835024 | tf_op jit(solution)/shard_map/all_gather | solution.py:42
  205.2 16.9 %fusion.26 = f32[512,2048]{1,0:T(8,128)} fusion(bf16[512,1792]{1,0:T(8,128)(2,1)} %all-gather.7.cloned.1.call-done, f32[1792,2048]{1,0:T(8,128)} %param.12), kind=kOutput, calls=%fused_computation.36 | convolution fusion | flops 22548578304 | bytes 20709376 | tf_op jit(solution)/shard_map/dot_general | solution.py:43
  222.1 0.0 copy-start.4
  222.1 0.0 all-reduce.2.cloned.1.call-update
  222.1 0.2 reduce-scatter.8.cloned.1.call-start
  222.3 103.0 %all-reduce.2.cloned.1.call-done = f32[512,2048]{1,0:T(8,128)} async-done(((f32[512,2048]{1,0:T(8,128)}), f32[512,2048]{1,0:T(8,128)}) %all-reduce.2.cloned.1.call-update) | async-done | bytes 4194320 | tf_op jit(solution)/shard_map/psum | solution.py:47
  325.3 0.0 copy-done.4
  325.3 4.9 fusion.24
  330.2 0.0 copy-start
  330.2 2.0 copy-done
  332.2 0.0 copy-start.3
  332.2 0.0 copy-start.5
  332.2 26.6 %fusion.27 = f32[512,1792]{1,0:T(8,128)} fusion(f32[512,2048]{1,0:T(8,128)S(1)} %get-tuple-element.7, f32[2048,1792]{1,0:T(8,128)} %param.14), kind=kOutput, calls=%fused_computation.37 | convolution fusion | flops 22548578304 | bytes 22544384 | tf_op jit(solution)/shard_map/dot_general | solution.py:51
  358.9 0.0 reduce-scatter.8.cloned.1.call-update
  358.9 0.0 all-gather.9.cloned.1.call-start
  359.0 45.1 %reduce-scatter.8.cloned.1.call-done = f32[64,1792]{1,0:T(8,128)} async-done(((f32[512,1792]{1,0:T(8,128)}), f32[64,1792]{1,0:T(8,128)}) %reduce-scatter.8.cloned.1.call-update) | async-done | bytes 458768 | tf_op jit(solution)/shard_map/reduce_scatter | solution.py:52
  404.0 0.0 copy-done.3
  404.0 0.0 copy-done.5
  404.0 1.8 multiply_convert_fusion
  405.8 0.0 all-gather.9.cloned.1.call-update
  405.8 0.3 all-gather.13.cloned.1.call-start
  406.1 25.6 %all-gather.9.cloned.1.call-done = bf16[512,1792]{1,0:T(8,128)(2,1)} async-done(((bf16[64,1792]{1,0:T(8,128)(2,1)}), bf16[512,1792]{1,0:T(8,128)(2,1)}) %all-gather.9.cloned.1.call-update) | async-done | bytes 1835024 | tf_op jit(solution)/shard_map/all_gather | solution.py:54
  431.7 16.5 %convolution_convert_fusion = bf16[512,2048]{1,0:T(8,128)(2,1)} fusion(bf16[512,1792]{1,0:T(8,128)(2,1)} %all-gather.9.cloned.1.call-done, f32[2048,1792]{1,0:T(8,128)} %param.14), kind=kOutput, calls=%fused_computation.15 | convolution fusion | flops 22549626880 | bytes 18612224 | tf_op jit(solution)/shard_map/dot_general | solution.py:58
  448.2 0.0 all-gather.13.cloned.1.call-update
  448.2 0.0 copy-start.2
  448.3 6.3 %multiply_reduce_fusion = f32[2048]{0:T(1024)S(1)} fusion(f32[2048,1792]{1,0:T(8,128)} %param.14), kind=kLoop, calls=%fused_computation.1 | loop fusion | flops 7337984 | bytes 14688256 | tf_op jit(solution)/shard_map/reduce_sum | solution.py:45
  454.6 0.1 broadcast_select_fusion
  454.7 17.1 %psum.15 = f32[2,2048]{1,0:T(2,128)S(1)} all-reduce(f32[2,2048]{1,0:T(2,128)S(1)} %broadcast_select_fusion), channel_id=1, replica_groups=mesh['mp'=2,'width'=2,'hidden'=8] {'mp','width'}, use_global_device_ids=true, to_apply=%region_6.7 | all-reduce | flops 4096 | bytes 32768 | tf_op jit(solution)/shard_map/psum | solution.py:47
  471.9 0.7 convert_bitcast_fusion
  472.6 0.0 copy-done.2
  472.6 0.9 convert_reduce_fusion
  473.5 18.9 %multiply_add_fusion = f32[2048,1792]{1,0:T(8,128)} fusion(f32[2048,1792]{1,0:T(8,128)} %param.14, f32[512,2048]{1,0:T(8,128)} %copy-done, bf16[512,1792]{1,0:T(8,128)(2,1)S(1)} %copy-done.2, f32[2048]{0:T(1024)S(1)} %divide_multiply_fusion.1), kind=kOutput, calls=%fused_computation | convolution fusion | flops 22555918336 | bytes 35397632 | tf_op jit(solution)/shard_map/dot_general | solution.py:71
  492.4 43.3 %all-gather.13.cloned.1.call-done = bf16[2048,2048]{1,0:T(8,128)(2,1)} async-done(((bf16[512,2048]{1,0:T(8,128)(2,1)}), bf16[2048,2048]{1,0:T(8,128)(2,1)}) %all-gather.13.cloned.1.call-update) | async-done | bytes 8388624 | tf_op jit(solution)/shard_map/all_gather | solution.py:15
  535.7 5.7 reduce_sum.48
  541.4 0.0 copy-start.1
  541.4 0.0 copy-start.7
  541.4 4.3 fusion.22
  545.7 0.0 copy-done.1
  545.7 0.0 copy-done.7
  545.7 15.6 %fusion.23 = f32[1792,2048]{1,0:T(8,128)} fusion(bf16[512,1792]{1,0:T(8,128)(2,1)S(1)} %copy-done.7, bf16[512,2048]{1,0:T(8,128)(2,1)S(1)} %reduce_sum.48, f32[512,2048]{1,0:T(8,128)S(1)} %copy-done.1, f32[2048]{0:T(1024)S(1)} %bitcast.35, f32[2048]{0:T(1024)S(1)} %copy-done.4), kind=kOutput, calls=%fused_computation.34 | convolution fusion | flops 22556966912 | bytes 22822912 | tf_op jit(solution)/shard_map/dot_general | solution.py:66
  (5 shorter events, 0.1 us)
Async XLA Ops:
  7.2 47.7 %all-gather.11.cloned.1.call-start = ((), (), s32[]{:S(2)}) async-start(), calls=%async_computation.9 | async-start | bytes 4128768 | tf_op jit(solution)/shard_map/all_gather | solution.py:27
  7.9 148.5 %reduce-scatter.4.cloned.1.call-start = ((), (), s32[]{:S(2)}) async-start(), calls=%async_computation.3 | async-start | bytes 8257536 | tf_op jit(solution)/shard_map/reduce_scatter | solution.py:34
  54.9 9.6 %copy-start.6 = (bf16[1,512,3584]{2,1,0:T(8,128)(2,1)S(1)}, bf16[1,512,3584]{2,1,0:T(8,128)(2,1)}, u32[]{:S(2)}) copy-start(bf16[1,512,3584]{2,1,0:T(8,128)(2,1)} %all-gather.11.cloned.1.call-done) | copy-start | bytes 11010052
  54.9 16.8 %slice-start = ((s8[6422528]{0:T(1024)(128)(4,1)}), s8[4194304]{0:T(1024)(128)(4,1)S(1)}, s32[]{:S(2)}) async-start(s8[6422528]{0:T(1024)(128)(4,1)} %bitcast.37), calls=%async_computation.11 | async-start | bytes 8388608
  64.6 7.2 %slice-start.1 = ((s8[6422528]{0:T(1024)(128)(4,1)}), s8[2228224]{0:T(1024)(128)(4,1)S(1)}, s32[]{:S(2)}) async-start(s8[6422528]{0:T(1024)(128)(4,1)} %bitcast.37), calls=%async_computation.12 | async-start | bytes 4456448
  77.8 98.3 %reduce-scatter.6.cloned.1.call-start = ((), (), s32[]{:S(2)}) async-start(), calls=%async_computation.4 | async-start | bytes 1376256 | tf_op jit(solution)/shard_map/reduce_scatter | solution.py:40
  156.4 48.8 %all-gather.7.cloned.1.call-start = ((), (), s32[]{:S(2)}) async-start(), calls=%async_computation.5 | async-start | bytes 2064384 | tf_op jit(solution)/shard_map/all_gather | solution.py:42
  177.9 147.5 %all-reduce.2.cloned.1.call-start = ((), (), s32[]{:S(2)}) async-start(), calls=%async_computation.6 | async-start | bytes 8388608 | tf_op jit(solution)/shard_map/psum | solution.py:47
  222.1 103.2 %copy-start.4 = (f32[2048]{0:T(1024)S(1)}, f32[2048]{0:T(1024)}, u32[]{:S(2)}) copy-start(f32[2048]{0:T(1024)} %param.13) | copy-start | bytes 24580
  222.1 181.9 %reduce-scatter.8.cloned.1.call-start = ((), (), s32[]{:S(2)}) async-start(), calls=%async_computation.7 | async-start | bytes 4128768 | tf_op jit(solution)/shard_map/reduce_scatter | solution.py:52
  330.2 2.0 copy-start
  332.2 71.8 %copy-start.3 = (f32[64,1792]{1,0:T(8,128)S(1)}, f32[64,1792]{1,0:T(8,128)}, u32[]{:S(2)}) copy-start(f32[64,1792]{1,0:T(8,128)} %reduce-scatter.6.cloned.1.call-done) | copy-start | bytes 1376260
  332.2 71.8 %copy-start.5 = (f32[1792]{0:T(1024)S(1)}, f32[1792]{0:T(1024)}, u32[]{:S(2)}) copy-start(f32[1792]{0:T(1024)} %param.15) | copy-start | bytes 21508
  358.9 72.7 %all-gather.9.cloned.1.call-start = ((), (), s32[]{:S(2)}) async-start(), calls=%async_computation.8 | async-start | bytes 2064384 | tf_op jit(solution)/shard_map/all_gather | solution.py:54
  405.8 129.8 %all-gather.13.cloned.1.call-start = ((), (), s32[]{:S(2)}) async-start(), calls=%async_computation.10 | async-start | bytes 10485760 | tf_op jit(solution)/shard_map/all_gather | solution.py:15
  448.2 24.3 %copy-start.2 = (bf16[512,1792]{1,0:T(8,128)(2,1)S(1)}, bf16[512,1792]{1,0:T(8,128)(2,1)}, u32[]{:S(2)}) copy-start(bf16[512,1792]{1,0:T(8,128)(2,1)} %all-gather.9.cloned.1.call-done) | copy-start | bytes 5505028
  541.4 4.3 copy-start.1
  541.4 4.3 copy-start.7
Sparse Core Ops, SparseCore 0:
  9.6 45.2 all-gather.10
  77.9 78.4 reduce-scatter.3
  158.7 17.3 reduce-scatter.5
  178.2 26.9 all-gather.6
  222.2 103.0 all-reduce.1
  359.0 44.9 reduce-scatter.7
  406.2 25.3 all-gather.8
  448.3 87.2 all-gather.12
